TPU v7x, 128 devices: a whole 4x4x4 slice. The times are simulated.
128 devices in a mesh: expert: 8 (over z_lo, x), shard: 16 (over z_hi, y, core).
Axes of the slice: x: 4, y: 4, z: 4 (z_hi: 2, z_lo: 2; z = z_hi * 2 + z_lo), core: 2. Of those that a mesh axis runs over, the one named last changes fastest.
Arguments:
- grad_out: bfloat16 [8, 2048, 3072], P('expert', 'shard'), may hold values from -6 to 6
- gate_pre: bfloat16 [8, 2048, 8192], P('expert', None, 'shard'), may hold values from -8 to 8
- up_pre: bfloat16 [8, 2048, 8192], P('expert', None, 'shard'), may hold values from -6 to 6
- counts: int32 [8, 16], P('expert', 'shard'), may hold values from 32 to 128
- placement: int32 [8], replicated, may hold values from 0 to 63, as said below
- master: float32 [8, 8192, 3072], P('expert', 'shard')
Outputs:
- d_gate: bfloat16 [8, 2048, 8192], P('expert', None, 'shard')
- d_up: bfloat16 [8, 2048, 8192], P('expert', None, 'shard')
- new_master: float32 [8, 8192, 3072], P('expert', 'shard')
Inputs may be any that keep to these rules, and one draw needn't show every extreme that they name: `placement`: slots that hold the same expert form aligned blocks of 1, 2 or 4 consecutive slots, each block starting at a multiple of its size; different blocks hold different experts.
All inputs are finite; a program needn't handle non-finite values.
Results may differ from a plain program's by a relative error of at most 0.006.
Values may be sent and summed in bfloat16 or wider, within the bound.
A program may use at most 256 MiB of HBM per device.

v0:
```python
import jax
import jax.numpy as jnp
from jax import lax
from jax.sharding import PartitionSpec as P

learn_rate = 0.02
rms_eps = 1e-06


def from_partner(shard, axis, bit):
    return lax.ppermute(shard, axis, [(i, i ^ 1 << bit) for i in range(lax.axis_size(axis))])


def per_device(grad_out, gate_pre, up_pre, counts, placement, master):
    weight_work = master[0].astype(jnp.bfloat16)
    local_rows = grad_out.shape[1]
    row_valid = (jnp.arange(local_rows, dtype=jnp.int32) < counts[0, 0]).astype(jnp.bfloat16)
    masked = grad_out[0] * row_valid[:, None]
    gate_val = gate_pre[0].astype(jnp.float32)
    up_val = up_pre[0].astype(jnp.float32)
    gate_sig = jax.nn.sigmoid(gate_val)
    gate_act = gate_val * gate_sig
    gate_slope = gate_sig * (1.0 + gate_val * (1.0 - gate_sig))
    hidden = (gate_act * up_val).astype(jnp.bfloat16)
    my_slot = lax.axis_index("expert")
    slot_order = jnp.arange(placement.shape[0], dtype=jnp.int32)
    my_expert = jnp.sum(jnp.where(slot_order == my_slot, placement, 0))
    block_rows = lax.all_gather(masked, "shard", axis=0, tiled=True)
    d_hidden = lax.dot_general(
        block_rows, weight_work, (((1,), (1,)), ((), ())), preferred_element_type=jnp.float32
    )
    up_acc = (d_hidden * gate_act).astype(jnp.bfloat16)
    gate_acc = (d_hidden * up_val * gate_slope).astype(jnp.bfloat16)
    grad_acc = lax.dot_general(
        hidden, block_rows, (((0,), (0,)), ((), ())), preferred_element_type=jnp.float32
    )
    grad_sum = grad_acc
    for bit_pos in range(2):
        received = from_partner(grad_sum.astype(jnp.bfloat16), "expert", bit_pos).astype(
            grad_sum.dtype
        )
        other_slot = jnp.bitwise_xor(my_slot, 1 << bit_pos)
        their_expert = jnp.sum(jnp.where(slot_order == other_slot, placement, 0))
        grad_sum = grad_sum + jnp.where(my_expert == their_expert, received, 0.0)
    row_rms = jnp.sqrt(jnp.mean(grad_sum * grad_sum, axis=1, keepdims=True) + rms_eps)
    new_master = master[0] - learn_rate * grad_sum / row_rms
    return (gate_acc[None], up_acc[None], new_master[None])


def solution(mesh):
    return jax.shard_map(
        per_device,
        mesh=mesh,
        in_specs=(
            P("expert", "shard", None),
            P("expert", None, "shard"),
            P("expert", None, "shard"),
            P("expert", "shard"),
            P(),
            P("expert", "shard", None),
        ),
        out_specs=(
            P("expert", None, "shard"),
            P("expert", None, "shard"),
            P("expert", "shard", None),
        ),
        check_vma=False,
    )
```

profile of v0, /device:TPU:0, one launch (start us, length us, event | category | flops | bytes accessed | tf_op | source)
XLA Modules:
  0.0 284.9 jit_solution(8563610116932885319)
XLA Ops:
  7.2 0.0 all-gather.2.cloned.1.call-start
  7.9 2.1 bitcast_multiply_fusion
  10.0 0.0 all-gather.2.cloned.1.call-update
  10.0 0.0 copy-start.2
  10.0 94.5 %all-gather.2.cloned.1.call-done = bf16[2048,3072]{1,0:T(8,128)(2,1)} async-done(((bf16[128,3072]{1,0:T(8,128)(2,1)}), bf16[2048,3072]{1,0:T(8,128)(2,1)}) %all-gather.2.cloned.1.call-update) | async-done | bytes 12582928 | tf_op jit(solution)/shard_map/all_gather | solution.py:28
  104.5 13.4 %fusion.21 = (bf16[512,3072]{1,0:T(8,128)(2,1)}, f32[512,3072]{1,0:T(8,128)}) fusion(bf16[2048,3072]{1,0:T(8,128)(2,1)} %all-gather.2.cloned.1.call-done, bf16[1,2048,512]{2,1,0:T(8,128)(2,1)} %param.8, bf16[1,2048,512]{2,1,0:T(8,128)(2,1)} %param.7), kind=kOutput, calls=%fused_computation.36 | convolution fusion | flops 6452412416 | bytes 26214400 | tf_op jit(solution)/shard_map/dot_general | solution.py:34
  117.9 1.5 collective-permute-start
  119.4 0.0 copy-done.2
  119.4 0.7 fusion.18
  121.5 66.9 %collective-permute-done = bf16[512,3072]{1,0:T(8,128)(2,1)S(1)} collective-permute-done((bf16[512,3072]{1,0:T(8,128)(2,1)}, bf16[512,3072]{1,0:T(8,128)(2,1)S(1)}, u32[]{:S(2)}, u32[]{:S(2)}) %collective-permute-start) | collective-permute-done | bytes 3145760 | tf_op jit(solution)/shard_map/ppermute | solution.py:11
  188.4 0.0 copy-start
  188.4 1.6 copy-done
  190.1 0.0 slice-start
  190.1 6.6 %fusion.9 = bf16[512,3072]{1,0:T(8,128)(2,1)} fusion(f32[512,3072]{1,0:T(8,128)} %get-tuple-element.9, bf16[512,3072]{1,0:T(8,128)(2,1)} %copy-done, pred[]{:T(512)S(6)} %eq.28), kind=kLoop, calls=%fused_computation.20 | loop fusion | flops 6291456 | bytes 12582913 | tf_op jit(solution)/shard_map/convert_element_type | solution.py:39
  196.6 3.0 %collective-permute-start.1 = (bf16[512,3072]{1,0:T(8,128)(2,1)}, bf16[512,3072]{1,0:T(8,128)(2,1)}, u32[]{:S(2)}, u32[]{:S(2)}) collective-permute-start(bf16[512,3072]{1,0:T(8,128)(2,1)} %fusion.9), channel_id=1, source_target_pairs={{0,32},{16,48},{32,0},{48,16},{64,96},{80,112},{96,64},{112,80},{1... | collective-permute-start | bytes 9437192 | tf_op jit(solution)/shard_map/ppermute | solution.py:11
  200.9 0.0 slice-start.1
  200.9 0.0 copy-start.1
  200.9 16.6 %fusion.11 = (bf16[1,2048,512]{2,1,0:T(8,128)(2,1)}, bf16[1,2048,512]{2,1,0:T(8,128)(2,1)}) fusion(bf16[1,2048,512]{2,1,0:T(8,128)(2,1)} %param.7, bf16[1,2048,512]{2,1,0:T(8,128)(2,1)} %param.8, bf16[2048,3072]{1,0:T(8,128)(2,1)} %all-gather.2.cloned.1.call-done, f32[1,512,3072]{2,1,0:T(8,128)} %param.11), kind=kOutput, calls=%fused_computation.22 | convolution fusion | flops 6458179584 | bytes 27262976 | tf_op jit(solution)/shard_map/dot_general | solution.py:29
  217.5 50.4 %collective-permute-done.1 = bf16[512,3072]{1,0:T(8,128)(2,1)} collective-permute-done((bf16[512,3072]{1,0:T(8,128)(2,1)}, bf16[512,3072]{1,0:T(8,128)(2,1)}, u32[]{:S(2)}, u32[]{:S(2)}) %collective-permute-start.1) | collective-permute-done | bytes 3145760 | tf_op jit(solution)/shard_map/ppermute | solution.py:11
  267.9 0.0 slice-done
  267.9 0.0 slice-done.1
  267.9 0.0 copy-done.1
  267.9 3.6 %multiply_reduce_fusion = f32[512]{0:T(512)S(1)} fusion(bf16[512,3072]{1,0:T(8,128)(2,1)} %collective-permute-done.1, pred[]{:T(512)S(6)} %eq.31, f32[512,3072]{1,0:T(8,128)S(1)} %bitcast.54, bf16[512,3072]{1,0:T(8,128)(2,1)S(1)} %copy-done.1, pred[]{:T(512)S(6)} %eq.28), kind=kLoop, calls=%fused_computation.6 | loop fusion | flops 12582400 | bytes 12584962 | tf_op jit(solution)/shard_map/reduce_sum | solution.py:45
  271.6 6.5 %fusion = f32[1,512,3072]{2,1,0:T(8,128)} fusion(f32[1,512,3072]{2,1,0:T(8,128)} %param.11, f32[512]{0:T(512)S(1)} %add_sqrt_fusion, bf16[512,3072]{1,0:T(8,128)(2,1)} %collective-permute-done.1, pred[]{:T(512)S(6)} %eq.31, f32[512,3072]{1,0:T(8,128)S(1)} %bitcast.54, bf16[512,3072]{1,0:T(8,128)(2,1)S(1)} %copy-done.1, pred[]{:T(512)S(6)} %eq.28), kind=kLoop, calls=%fused_computation.5 | loop fusion | flops 14155776 | bytes 25167874 | tf_op jit(solution)/shard_map/broadcast_in_dim | solution.py:47
  (3 shorter events, 0.0 us)
Async XLA Ops:
  7.2 97.4 %all-gather.2.cloned.1.call-start = ((), (), s32[]{:S(2)}) async-start(), calls=%async_computation | async-start | bytes 13369344 | tf_op jit(solution)/shard_map/all_gather | solution.py:28
  10.0 109.4 %copy-start.2 = (s32[8]{0:T(128)S(1)}, s32[8]{0:T(128)}, u32[]{:S(2)}) copy-start(s32[8]{0:T(128)} %param.10) | copy-start | bytes 100
  117.9 70.5 %collective-permute-start = (bf16[512,3072]{1,0:T(8,128)(2,1)}, bf16[512,3072]{1,0:T(8,128)(2,1)S(1)}, u32[]{:S(2)}, u32[]{:S(2)}) collective-permute-start(bf16[512,3072]{1,0:T(8,128)(2,1)} %get-tuple-element.8), channel_id=1, source_target_pairs={{0,16},{16,0},{32,48},{48,32},{64,80},{80,64},{96,112},{112,96},{1... | collective-permute-start | bytes 9437192 | tf_op jit(solution)/shard_map/ppermute | solution.py:11
  188.4 1.6 copy-start
  190.1 77.8 %slice-start = ((s8[6291456]{0:T(1024)(128)(4,1)}), s8[2097152]{0:T(1024)(128)(4,1)S(1)}, s32[]{:S(2)}) async-start(s8[6291456]{0:T(1024)(128)(4,1)} %bitcast.53), calls=%async_computation.1 | async-start | bytes 4194304
  196.6 71.3 %collective-permute-start.1 = (bf16[512,3072]{1,0:T(8,128)(2,1)}, bf16[512,3072]{1,0:T(8,128)(2,1)}, u32[]{:S(2)}, u32[]{:S(2)}) collective-permute-start(bf16[512,3072]{1,0:T(8,128)(2,1)} %fusion.9), channel_id=1, source_target_pairs={{0,32},{16,48},{32,0},{48,16},{64,96},{80,112},{96,64},{112,80},{1... | collective-permute-start | bytes 9437192 | tf_op jit(solution)/shard_map/ppermute | solution.py:11
  200.9 67.0 %slice-start.1 = ((s8[6291456]{0:T(1024)(128)(4,1)}), s8[4194304]{0:T(1024)(128)(4,1)S(1)}, s32[]{:S(2)}) async-start(s8[6291456]{0:T(1024)(128)(4,1)} %bitcast.53), calls=%async_computation.2 | async-start | bytes 8388608
  200.9 67.0 %copy-start.1 = (bf16[512,3072]{1,0:T(8,128)(2,1)S(1)}, bf16[512,3072]{1,0:T(8,128)(2,1)}, u32[]{:S(2)}) copy-start(bf16[512,3072]{1,0:T(8,128)(2,1)} %copy-done) | copy-start | bytes 9437188
Sparse Core Ops, SparseCore 0:
  11.0 93.4 all-gather.1
where the time goes:
time: 285 us
  waiting for transfers between devices  212 us (74%)
  matrix products  30 us (11%)
  other arithmetic  19.6 us (7%)
  between operations  17.4 us (6%)
  starting transfers between devices  4.49 us (2%)
    ppermute x2, waiting for transfers between devices, from_partner(): lax.ppermute(shard, axis, [(i, i ^ 1 << bit) for i in range(lax.axis_size...  117 us
    all_gather x1, waiting for transfers between devices, per_device(): block_rows = lax.all_gather(masked, 'shard', axis=0, tiled=True)  94.5 us
    dot_general x1, matrix products, per_device(): lax.dot_general(block_rows, weight_work, (((1,), (1,)), ((), ())), prefer...  16.6 us
    dot_general x1, matrix products, per_device(): lax.dot_general(hidden, block_rows, (((0,), (0,)), ((), ())), preferred_e...  13.4 us
    convert_element_type x1, other arithmetic, per_device(): grad_sum.astype(jnp.bfloat16)  6.56 us
    broadcast_in_dim x1, other arithmetic, per_device(): return (gate_acc[None], up_acc[None], new_master[None])  6.48 us
  transfers between devices with their start and end apart: 3, of which 3 were waited for; matrix products, arithmetic and copies ran while one was open for 6% of the time, Pallas kernels for 0%

commit v1 on v0

--- a/solution.py
+++ b/solution.py
@@ -25,7 +25,9 @@
     my_slot = lax.axis_index("expert")
     slot_order = jnp.arange(placement.shape[0], dtype=jnp.int32)
     my_expert = jnp.sum(jnp.where(slot_order == my_slot, placement, 0))
-    block_rows = lax.all_gather(masked, "shard", axis=0, tiled=True)
+    block_rows = jnp.concatenate(
+        lax.all_to_all(jnp.stack([masked] * lax.axis_size("shard")), "shard", 0, 0), axis=0
+    )
     d_hidden = lax.dot_general(
         block_rows, weight_work, (((1,), (1,)), ((), ())), preferred_element_type=jnp.float32
     )

time: 285 us -> 327 us (1.15)
  blocking collectives: 0 us -> 150 us
  waiting for transfers between devices: 212 us -> 115 us
  between operations: 17.4 us -> 3.98 us
  local copies, waits for them, and re-layouts: 1.67 us -> 7.88 us
  matrix products: 30 us -> 26.3 us
    all_to_all x0 -> x1, blocking collectives: none -> 150 us  [per_device(): lax.all_to_all(jnp.stack([masked] * lax.axis_size('shard')), 'shard', 0, 0)]
    all_gather x1 -> x0, waiting for transfers between devices: 94.5 us -> none  [per_device(): block_rows = lax.all_gather(masked, 'shard', axis=0, tiled=True)]
    another operation x0 -> x1, local copies, waits for them, and re-layouts: none -> 6.21 us  [per_device(): jnp.stack([masked] * lax.axis_size('shard'))]
    dot_general x1, matrix products: 13.4 us -> 9.65 us  [per_device(): lax.dot_general(hidden, block_rows, (((0,), (0,)), ((), ())), preferred_e...]
  transfers between devices with their start and end apart: 3 -> 2, of which waited for: 3 -> 2; matrix products, arithmetic and copies ran while one was open for 6% -> 5% of each run, Pallas kernels for 0% -> 0%
where the time goes in v1:
time: 327 us
  blocking collectives  150 us (46%)
  waiting for transfers between devices  115 us (35%)
  matrix products  26.3 us (8%)
  other arithmetic  18.7 us (6%)
  local copies, waits for them, and re-layouts  7.88 us (2%)
  starting transfers between devices  4.51 us (1%)
  between operations  3.98 us (1%)
    all_to_all x1, blocking collectives, per_device(): lax.all_to_all(jnp.stack([masked] * lax.axis_size('shard')), 'shard', 0, 0)  150 us
    ppermute x2, waiting for transfers between devices, from_partner(): lax.ppermute(shard, axis, [(i, i ^ 1 << bit) for i in range(lax.axis_size...  115 us
    dot_general x1, matrix products, per_device(): lax.dot_general(block_rows, weight_work, (((1,), (1,)), ((), ())), prefer...  16.6 us
    dot_general x1, matrix products, per_device(): lax.dot_general(hidden, block_rows, (((0,), (0,)), ((), ())), preferred_e...  9.65 us
    convert_element_type x1, other arithmetic, per_device(): grad_sum.astype(jnp.bfloat16)  6.56 us
  transfers between devices with their start and end apart: 2, of which 2 were waited for; matrix products, arithmetic and copies ran while one was open for 5% of the time, Pallas kernels for 0%

profile of v1, /device:TPU:0, one launch (start us, length us, event | category | flops | bytes accessed | tf_op | source)
XLA Modules:
  0.0 326.6 jit_solution(9414034670711462292)
XLA Ops:
  1.3 1.3 multiply_bitcast_fusion
  2.5 6.2 %stack.5 = bf16[16,128,3072]{2,1,0:T(8,128)(2,1)} broadcast(bf16[128,3072]{1,0:T(8,128)(2,1)S(1)} %multiply_bitcast_fusion), dimensions={1,2} | broadcast | bytes 13369344 | tf_op jit(solution)/shard_map/stack | solution.py:29
  8.8 0.0 copy-start.4
  8.8 149.8 %all_to_all.5 = bf16[16,128,3072]{2,1,0:T(8,128)(2,1)S(1)} all-to-all(bf16[16,128,3072]{2,1,0:T(8,128)(2,1)} %stack.5), channel_id=1, replica_groups=mesh['expert'=8,'shard'=16] {'shard'}, dimensions={0} | all-to-all | bytes 25165824 | tf_op jit(solution)/shard_map/all_to_all | solution.py:29
  158.6 0.0 copy-done.4
  158.6 0.0 copy-done.5
  158.6 9.6 %fusion.31 = (bf16[512,3072]{1,0:T(8,128)(2,1)}, f32[512,3072]{1,0:T(8,128)}) fusion(bf16[2048,3072]{1,0:T(8,128)(2,1)S(1)} %bitcast.71, bf16[1,2048,512]{2,1,0:T(8,128)(2,1)S(1)} %copy-done.5, bf16[1,2048,512]{2,1,0:T(8,128)(2,1)S(1)} %copy-done.4), kind=kOutput, calls=%fused_computation.45 | convolution fusion | flops 6452412416 | bytes 26214400 | tf_op jit(solution)/shard_map/dot_general | solution.py:36
  168.2 0.0 copy-done.2
  168.2 1.5 collective-permute-start
  169.7 0.0 copy-done.3
  169.7 0.7 fusion.29
  171.8 66.1 %collective-permute-done = bf16[512,3072]{1,0:T(8,128)(2,1)S(1)} collective-permute-done((bf16[512,3072]{1,0:T(8,128)(2,1)}, bf16[512,3072]{1,0:T(8,128)(2,1)S(1)}, u32[]{:S(2)}, u32[]{:S(2)}) %collective-permute-start) | collective-permute-done | bytes 3145760 | tf_op jit(solution)/shard_map/ppermute | solution.py:11
  237.9 1.6 copy-done
  239.5 6.6 %fusion.18 = bf16[512,3072]{1,0:T(8,128)(2,1)} fusion(f32[512,3072]{1,0:T(8,128)} %get-tuple-element.9, bf16[512,3072]{1,0:T(8,128)(2,1)} %copy-done, pred[]{:T(512)S(6)} %eq.28), kind=kLoop, calls=%fused_computation.27 | loop fusion | flops 6291456 | bytes 12582913 | tf_op jit(solution)/shard_map/convert_element_type | solution.py:41
  246.1 3.0 collective-permute-start.1
  250.4 0.0 slice-start.1
  250.4 0.0 copy-start.1
  250.4 16.6 %fusion.25 = (bf16[1,2048,512]{2,1,0:T(8,128)(2,1)}, bf16[1,2048,512]{2,1,0:T(8,128)(2,1)}) fusion(bf16[1,2048,512]{2,1,0:T(8,128)(2,1)} %param.7, bf16[1,2048,512]{2,1,0:T(8,128)(2,1)} %param.8, bf16[2048,3072]{1,0:T(8,128)(2,1)} %bitcast.72, f32[1,512,3072]{2,1,0:T(8,128)} %param.11), kind=kOutput, calls=%fused_computation.33 | convolution fusion | flops 6459752448 | bytes 27262976 | tf_op jit(solution)/shard_map/dot_general | solution.py:31
  267.1 49.4 %collective-permute-done.1 = bf16[512,3072]{1,0:T(8,128)(2,1)} collective-permute-done((bf16[512,3072]{1,0:T(8,128)(2,1)}, bf16[512,3072]{1,0:T(8,128)(2,1)}, u32[]{:S(2)}, u32[]{:S(2)}) %collective-permute-start.1) | collective-permute-done | bytes 3145760 | tf_op jit(solution)/shard_map/ppermute | solution.py:11
  316.4 0.0 slice-done
  316.4 0.0 slice-done.1
  316.4 0.0 copy-done.1
  316.4 3.6 %multiply_reduce_fusion = f32[512]{0:T(512)S(1)} fusion(bf16[512,3072]{1,0:T(8,128)(2,1)} %collective-permute-done.1, pred[]{:T(512)S(6)} %eq.31, f32[512,3072]{1,0:T(8,128)S(1)} %bitcast.70, bf16[512,3072]{1,0:T(8,128)(2,1)S(1)} %copy-done.1, pred[]{:T(512)S(6)} %eq.28), kind=kLoop, calls=%fused_computation.8 | loop fusion | flops 12582400 | bytes 12584962 | tf_op jit(solution)/shard_map/reduce_sum | solution.py:47
  320.1 6.5 %fusion = f32[1,512,3072]{2,1,0:T(8,128)} fusion(f32[1,512,3072]{2,1,0:T(8,128)} %param.11, f32[512]{0:T(512)S(1)} %add_sqrt_fusion, bf16[512,3072]{1,0:T(8,128)(2,1)} %collective-permute-done.1, pred[]{:T(512)S(6)} %eq.31, f32[512,3072]{1,0:T(8,128)S(1)} %bitcast.70, bf16[512,3072]{1,0:T(8,128)(2,1)S(1)} %copy-done.1, pred[]{:T(512)S(6)} %eq.28), kind=kLoop, calls=%fused_computation.1 | loop fusion | flops 14155776 | bytes 25167874 | tf_op jit(solution)/shard_map/broadcast_in_dim | solution.py:49
  (8 shorter events, 0.0 us)
Async XLA Ops:
  8.8 149.8 %copy-start.4 = (bf16[1,2048,512]{2,1,0:T(8,128)(2,1)S(1)}, bf16[1,2048,512]{2,1,0:T(8,128)(2,1)}, u32[]{:S(2)}) copy-start(bf16[1,2048,512]{2,1,0:T(8,128)(2,1)} %param.7) | copy-start | bytes 6291460
  8.8 149.8 %copy-start.5 = (bf16[1,2048,512]{2,1,0:T(8,128)(2,1)S(1)}, bf16[1,2048,512]{2,1,0:T(8,128)(2,1)}, u32[]{:S(2)}) copy-start(bf16[1,2048,512]{2,1,0:T(8,128)(2,1)} %param.8) | copy-start | bytes 6291460
  158.6 9.7 %copy-start.2 = (bf16[16,128,3072]{2,1,0:T(8,128)(2,1)}, bf16[16,128,3072]{2,1,0:T(8,128)(2,1)S(1)}, u32[]{:S(2)}) copy-start(bf16[16,128,3072]{2,1,0:T(8,128)(2,1)S(1)} %all_to_all.5) | copy-start | bytes 37748740
  158.6 11.2 %copy-start.3 = (s32[8]{0:T(128)S(1)}, s32[8]{0:T(128)}, u32[]{:S(2)}) copy-start(s32[8]{0:T(128)} %param.10) | copy-start | bytes 100
  168.2 69.6 %collective-permute-start = (bf16[512,3072]{1,0:T(8,128)(2,1)}, bf16[512,3072]{1,0:T(8,128)(2,1)S(1)}, u32[]{:S(2)}, u32[]{:S(2)}) collective-permute-start(bf16[512,3072]{1,0:T(8,128)(2,1)} %get-tuple-element.8), channel_id=1, source_target_pairs={{0,16},{16,0},{32,48},{48,32},{64,80},{80,64},{96,112},{112,96},{1... | collective-permute-start | bytes 9437192 | tf_op jit(solution)/shard_map/ppermute | solution.py:11
  237.9 1.6 copy-start
  239.5 76.9 %slice-start = ((s8[6291456]{0:T(1024)(128)(4,1)}), s8[2097152]{0:T(1024)(128)(4,1)S(1)}, s32[]{:S(2)}) async-start(s8[6291456]{0:T(1024)(128)(4,1)} %bitcast.69), calls=%async_computation.1 | async-start | bytes 4194304
  246.1 70.3 %collective-permute-start.1 = (bf16[512,3072]{1,0:T(8,128)(2,1)}, bf16[512,3072]{1,0:T(8,128)(2,1)}, u32[]{:S(2)}, u32[]{:S(2)}) collective-permute-start(bf16[512,3072]{1,0:T(8,128)(2,1)} %fusion.18), channel_id=1, source_target_pairs={{0,32},{16,48},{32,0},{48,16},{64,96},{80,112},{96,64},{112,80},{1... | collective-permute-start | bytes 9437192 | tf_op jit(solution)/shard_map/ppermute | solution.py:11
  250.4 66.0 %slice-start.1 = ((s8[6291456]{0:T(1024)(128)(4,1)}), s8[4194304]{0:T(1024)(128)(4,1)S(1)}, s32[]{:S(2)}) async-start(s8[6291456]{0:T(1024)(128)(4,1)} %bitcast.69), calls=%async_computation.2 | async-start | bytes 8388608
  250.4 66.0 %copy-start.1 = (bf16[512,3072]{1,0:T(8,128)(2,1)S(1)}, bf16[512,3072]{1,0:T(8,128)(2,1)}, u32[]{:S(2)}) copy-start(bf16[512,3072]{1,0:T(8,128)(2,1)} %copy-done) | copy-start | bytes 9437188
